TPU v7x, 32 devices: a whole 2x2x4 slice. The times are simulated.
32 devices in a mesh: cuts: 2 (over x), outer: 16 (over z, y, core).
Axes of the slice: x: 2, y: 2, z: 4, core: 2. Of those that a mesh axis runs over, the one named last changes fastest.
Arguments:
- stem_tensor: bfloat16 [32, 512, 2, 512], P(('cuts', 'outer')), parts along dimension 0, may hold values from -6 to 6
- leaf_left: bfloat16 [4, 2, 8192, 2, 512], P(None, None, 'outer'), may hold values from -0.09375 to 0.09375
- leaf_right: bfloat16 [4, 2, 8192, 2, 512], P(None, None, 'outer'), may hold values from -0.125 to 0.125
- slice_bits: int32 [8], P('cuts'), parts along dimension 0, may hold values from 0 to 1, as said below
Outputs:
- stem_out: bfloat16 [32, 512, 2, 512], P(('cuts', 'outer')), parts along dimension 0
There are 2 independent parts, one for each index of `cuts`. A program takes and returns all parts, laid end to end along the dimension named above; an argument that names none is the same for every part. Nothing has to cross between parts.
Inputs may be any that keep to these rules, and one draw needn't show every extreme that they name: `slice_bits`: the first entry is the index of the part modulo 2, so neighbouring parts contract different slices; the other entries are drawn independently.
All inputs are finite; a program needn't handle non-finite values.
Results may differ from a plain program's by a relative error of at most 0.01.
Values may be sent and summed in bfloat16 or wider, within the bound.
A program may use at most 64 MiB of HBM per device.

v0:
```python
import functools

import jax
import jax.numpy as jnp
from jax import lax
from jax.experimental import pallas as pl
from jax.experimental.pallas import tpu as pltpu
from jax.sharding import PartitionSpec as P

ROUNDS = 2
TILES = 4
LAG = 2
EARLY = 14
SPREAD = 0.1
UNITS = 4
MESH = pl.DeviceIdType.MESH


def network_kernel(
    n, part, blocks0, out, acc, outgoing, incoming, branch, got0, got1, blocks1, absorbed,
    a_send, a_recv, r_send, r_recv,
):
    chunks, _, span, columns = part.shape
    planes = chunks // ROUNDS
    width = n * span
    steps = n.bit_length() - 1
    tiles = TILES
    group = n // tiles
    me = lax.axis_index("outer")
    high, low = me // group, lax.rem(me, group)

    barrier = pltpu.get_barrier_semaphore()

    def greet(k, carry):
        pl.semaphore_signal(barrier, inc=1, device_id={"outer": lax.rem(me + k, n)}, device_id_type=MESH)
        return carry

    lax.fori_loop(1, n, greet, 0)
    pl.semaphore_wait(barrier, n - 1)

    bits = [lax.rem(me // (1 << s), 2) for s in range(steps)]
    peers = [me + (1 << s) * (1 - 2 * bits[s]) for s in range(steps)]
    starts = [0]
    gives = []
    for s in range(steps):
        half = n >> (s + 1)
        gives.append(starts[s] + (1 - bits[s]) * half)
        starts.append(starts[s] + bits[s] * half)

    def copy_to(r, i, j):
        to = lax.rem(high + i, tiles) * group + lax.rem(low + j, group)
        k = i * group + j
        blocks, got = ((blocks0, got0), (blocks1, got1))[r]
        return pltpu.make_async_remote_copy(
            src_ref=blocks.at[to], dst_ref=got.at[me], send_sem=a_send.at[r, k], recv_sem=a_recv.at[r, k],
            device_id={"outer": to}, device_id_type=MESH)

    def copy_from(r, i, j):
        origin = lax.rem(high + tiles - i, tiles) * group + lax.rem(low + group - j, group)
        k = i * group + j
        blocks, got = ((blocks0, got0), (blocks1, got1))[r]
        return pltpu.make_async_remote_copy(
            src_ref=blocks.at[origin], dst_ref=got.at[origin], send_sem=a_send.at[r, k], recv_sem=a_recv.at[r, k],
            device_id={"outer": origin}, device_id_type=MESH)

    def over(i, act):
        def one(j, carry):
            act(i, j)
            return carry

        lax.fori_loop(1 if i == 0 else 0, group, one, 0)

    def reduce_copy(c, s):
        half, at = n >> (s + 1), n - (n >> s)
        return pltpu.make_async_remote_copy(
            src_ref=outgoing.at[c, pl.ds(gives[s], half)], dst_ref=incoming.at[c, pl.ds(at, half)],
            send_sem=r_send.at[c, s], recv_sem=r_recv.at[c, s],
            device_id={"outer": peers[s]}, device_id_type=MESH)

    def gather_copy(c, s, first):
        here = branch.at[c, pl.ds(first, n >> (s + 1))]
        return pltpu.make_async_remote_copy(
            src_ref=here, dst_ref=here, send_sem=r_send.at[c, 2 * steps - 1 - s], recv_sem=r_recv.at[c, 2 * steps - 1 - s],
            device_id={"outer": peers[s]}, device_id_type=MESH)

    def begin(c, step):
        if step < steps:
            give = pl.ds(gives[step], n >> (step + 1))
            source = acc if step else part
            outgoing[c, give] = source[c, give].astype(outgoing.dtype)
            reduce_copy(c, step).start()
        else:
            s = 2 * steps - 1 - step
            gather_copy(c, s, starts[s + 1]).start()

    def finish(c, step):
        if step < steps:
            half, at = n >> (step + 1), n - (n >> step)
            reduce_copy(c, step).wait_recv()
            keep = pl.ds(starts[step + 1], half)
            source = acc if step else part
            total = source[c, keep] + incoming[c, pl.ds(at, half)].astype(jnp.float32)
            if step == steps - 1:
                branch[c, keep] = total.astype(branch.dtype)
            else:
                acc[c, keep] = total
        else:
            s = 2 * steps - 1 - step
            gather_copy(c, s, gives[s]).wait_recv()

    def dot(a, b):
        return jnp.dot(a, b, preferred_element_type=jnp.float32)

    def absorb(r, i):
        got = (got0, got1)[r]
        over(i, lambda i, j: copy_from(r, i, j).wait_recv())
        here = pl.ds(lax.rem(high + tiles - i, tiles) * group, group)
        entries = got[here].reshape(group * 2 * span, columns)
        first = r * planes
        by_real = dot(entries, branch[first + 2].reshape(width, columns)).reshape(group, 2, span, columns)
        by_imag = dot(entries, branch[first + 3].reshape(width, columns)).reshape(group, 2, span, columns)
        absorbed[0, here] = (by_real[:, 0] - by_imag[:, 1]).astype(absorbed.dtype)
        absorbed[1, here] = (by_imag[:, 0] + by_real[:, 1]).astype(absorbed.dtype)

    def contract(r, where):
        here = pl.ds(where * group, group)
        first = r * planes
        p_real = branch[first, here].reshape(group * span, width)
        p_imag = branch[first + 1, here].reshape(group * span, width)
        a_real, a_imag = absorbed[0].reshape(width, columns), absorbed[1].reshape(width, columns)
        real_part = (dot(p_real, a_real) - dot(p_imag, a_imag)).astype(jnp.bfloat16)
        imag_part = (dot(p_real, a_imag) + dot(p_imag, a_real)).astype(jnp.bfloat16)
        return here, real_part.reshape(group, span, columns), imag_part.reshape(group, span, columns)

    def renew(i):
        here, real_part, imag_part = contract(0, lax.rem(high + i, tiles))
        blocks1[here, 0:span] = real_part
        blocks1[here, span : 2 * span] = imag_part
        if i == 0:
            got1[me] = blocks1[me]
        over(i, lambda i, j: copy_to(1, i, j).start())

    got0[me] = blocks0[me]
    order = [2, 1, 3, 0]
    sends = [(i, j) for i in order for j in range(group) if i or j]
    ready = planes - 1 + 2 * steps * LAG
    turn = [(c + planes // 2) % planes for c in range(planes)]
    entry = turn + [max(planes, ready - EARLY) + at for at in turn]
    work = [functools.partial(absorb, 0, i) for i in order] + [functools.partial(renew, i) for i in order]
    unsent = list(order)
    total_slots = max(entry) + 2 * steps * LAG + 1
    for t in range(total_slots):
        for c in range(chunks):
            if t < entry[c] or (t - entry[c]) % LAG:
                continue
            step = (t - entry[c]) // LAG
            if 1 <= step <= 2 * steps:
                finish(c, step - 1)
            if step < 2 * steps:
                begin(c, step)
        if unsent and t % max(1, int(ready * SPREAD) // tiles) == 0:
            over(unsent.pop(0), lambda i, j: copy_to(0, i, j).start())
        if t >= ready:
            assert not unsent
            for job in work[:UNITS]:
                job()
            work = work[UNITS:]
    assert not work

    for i in order:
        absorb(1, i)
    for where in range(tiles):
        here, real_part, imag_part = contract(1, where)
        out[0, here] = real_part
        out[1, here] = imag_part

    for r in range(2):
        for i in order:
            over(i, lambda i, j: copy_to(r, i, j).wait_send())
    for c in range(chunks):
        for s in range(steps):
            reduce_copy(c, s).wait_send()
            gather_copy(c, s, starts[s + 1]).wait_send()


def contract_network(n, part, blocks):
    chunks, _, span, columns = part.shape
    steps = n.bit_length() - 1
    both = part.shape
    vmem = pl.BlockSpec(memory_space=pltpu.VMEM)
    return pl.pallas_call(
        functools.partial(network_kernel, n),
        out_shape=jax.ShapeDtypeStruct((2, n, span, columns), jnp.bfloat16),
        in_specs=[vmem, vmem],
        out_specs=vmem,
        scratch_shapes=[
            pltpu.VMEM(both, jnp.float32),
            pltpu.VMEM(both, jnp.bfloat16),
            pltpu.VMEM(both, jnp.bfloat16),
            pltpu.VMEM(both, jnp.bfloat16),
            pltpu.VMEM(blocks.shape, jnp.bfloat16),
            pltpu.VMEM(blocks.shape, jnp.bfloat16),
            pltpu.VMEM(blocks.shape, jnp.bfloat16),
            pltpu.VMEM((2, n, span, columns), jnp.bfloat16),
            pltpu.SemaphoreType.DMA((2, n)),
            pltpu.SemaphoreType.DMA((2, n)),
            pltpu.SemaphoreType.DMA((chunks, 2 * steps)),
            pltpu.SemaphoreType.DMA((chunks, 2 * steps)),
        ],
        compiler_params=pltpu.CompilerParams(collective_id=0, has_side_effects=True),
    )(part, blocks)


def leaf_product(plain_ref, other_ref, out_ref):
    rows = 2 * plain_ref.shape[2]
    plain = plain_ref[0, 0].reshape(rows, plain_ref.shape[4])
    other = other_ref[0, 0].reshape(rows, other_ref.shape[4]).astype(jnp.float32)
    even = lax.rem(lax.broadcasted_iota(jnp.int32, other.shape, 0), 2) == 0
    signed = jnp.where(even, other, -other).astype(jnp.bfloat16)
    swapped = jnp.where(even, pltpu.roll(other, rows - 1, 0), pltpu.roll(other, 1, 0)).astype(jnp.bfloat16)
    dims = (((0,), (0,)), ((), ()))
    out_ref[0, 0] = lax.dot_general(plain, signed, dims, preferred_element_type=jnp.float32)
    out_ref[0, 1] = lax.dot_general(plain, swapped, dims, preferred_element_type=jnp.float32)


def leaf_kernel(bits, left_ref, right_ref, out_ref):
    transposed = lax.rem(pl.program_id(0), 2) == 0

    @pl.when(transposed)
    def _():
        leaf_product(right_ref, left_ref, out_ref)

    @pl.when(jnp.logical_not(transposed))
    def _():
        leaf_product(left_ref, right_ref, out_ref)


def leaf_terms(bits, leaf_left, leaf_right):
    branches, _, depth, _, row_count = leaf_left.shape
    width = leaf_right.shape[4]

    def chosen(j, chosen_bits):
        return (j, chosen_bits[j], 0, 0, 0)

    return pl.pallas_call(
        leaf_kernel,
        out_shape=jax.ShapeDtypeStruct((branches, 2, row_count, width), jnp.float32),
        grid_spec=pltpu.PrefetchScalarGridSpec(
            num_scalar_prefetch=1,
            grid=(branches,),
            in_specs=[
                pl.BlockSpec((1, 1, depth, 2, row_count), chosen),
                pl.BlockSpec((1, 1, depth, 2, width), chosen),
            ],
            out_specs=pl.BlockSpec((1, 2, row_count, width), lambda j, chosen_bits: (j, 0, 0, 0)),
        ),
    )(bits, leaf_left, leaf_right)


def on_device(n, stem_tensor, leaf_left, leaf_right, slice_bits):
    width, columns = stem_tensor.shape[1], stem_tensor.shape[3]
    span = width // n
    blocks = jnp.transpose(stem_tensor.reshape(n, span, 2, columns), (0, 2, 1, 3)).reshape(n, 2 * span, columns)
    part = leaf_terms(slice_bits, leaf_left, leaf_right).reshape(-1, n, span, columns)
    state = contract_network(n, part, blocks).reshape(2, width, columns)
    return jnp.transpose(state, (1, 0, 2))[None]


def solution(mesh):
    return jax.shard_map(
        functools.partial(on_device, mesh.shape["outer"]),
        mesh=mesh,
        in_specs=(
            P(("cuts", "outer"), None, None, None),
            P(None, None, "outer", None, None),
            P(None, None, "outer", None, None),
            P("cuts"),
        ),
        out_specs=P(("cuts", "outer"), None, None, None),
        check_vma=False,
    )
```

profile of v0, /device:TPU:1, one launch (start us, length us, event | category | flops | bytes accessed | tf_op | source)
XLA Modules:
  0.0 111.6 jit_solution(9103259699349880106)
XLA Ops:
  0.0 2.4 %copy.5 = bf16[16,32,2,512]{3,1,2,0:T(8,128)(2,1)} copy(bf16[16,32,2,512]{3,2,1,0:T(2,128)(2,1)} %bitcast.14) | data formatting | bytes 2097152 | tf_op jit(solution)/shard_map/reshape | solution.py:263
  2.4 11.6 %shard_map.46 = f32[4,2,512,512]{3,2,1,0:T(8,128)} custom-call(s32[4]{0:T(128)} %bits.1, bf16[4,2,512,2,512]{4,3,2,1,0:T(2,128)(2,1)} %left_ref.1, bf16[4,2,512,2,512]{4,3,2,1,0:T(2,128)(2,1)} %right_ref.1), custom_call_target="tpu_custom_call" | custom-call | tf_op jit(solution)/shard_map/pallas_call | solution.py:245
  14.1 94.2 %shard_map.47 = bf16[2,16,32,512]{3,2,1,0:T(8,128)(2,1)} custom-call(f32[8,16,32,512]{3,2,1,0:T(8,128)} %bitcast.11, bf16[16,64,512]{2,1,0:T(8,128)(2,1)} %bitcast.13), custom_call_target="tpu_custom_call" | custom-call | tf_op jit(solution)/shard_map/pallas_call | solution.py:191
  108.3 3.3 %copy.8 = bf16[2,512,512]{2,0,1:T(2,128)(2,1)} copy(bf16[2,512,512]{2,1,0:T(8,128)(2,1)} %bitcast.12) | data formatting | bytes 2097152 | tf_op jit(solution)/shard_map/reshape | solution.py:265
where the time goes:
time: 113 us; the launch traced here: 112 us
  Pallas kernels  106 us (94%)
  local copies, waits for them, and re-layouts  5.69 us (5%)
    pallas_call x1, Pallas kernels, contract_network(): pl.pallas_call(functools.partial(network_kernel, n), out_shape=jax.ShapeD...  94.2 us
    pallas_call x1, Pallas kernels, leaf_terms(): pl.pallas_call(leaf_kernel, out_shape=jax.ShapeDtypeStruct((branches, 2,...  11.6 us
    reshape x1, local copies, waits for them, and re-layouts, on_device(): state = contract_network(n, part, blocks).reshape(2, width, columns)  3.27 us
    reshape x1, local copies, waits for them, and re-layouts, on_device(): stem_tensor.reshape(n, span, 2, columns)  2.42 us

commit v1 on v0

v1 whole, which is shorter than its diff:
```python
import functools

import jax
import jax.numpy as jnp
from jax import lax
from jax.experimental import pallas as pl
from jax.experimental.pallas import tpu as pltpu
from jax.sharding import PartitionSpec as P

MESH = pl.DeviceIdType.MESH
LANES = 128
STAGES = (1.6, 4.5, 3.5, 3.5)
ENTRIES = {0: 5.0, 2: 10.0, 1: 15.0, 3: 20.0}
PLANE_GAP = 0.4
LEAVES = {0: 3.0, 2: 6.0, 1: 9.5, 3: 13.0}
FIRST_SENDS = (2.0, 4.9, 9.0, 14.0)
SPLITS = (15.0, 18.0, 21.0, 24.0)


def network_kernel(
    n, bits, stem, left, right, out,
    l0, l1, l2, l3, r0, r1, r2, r3, part, outgoing, incoming, branch, got0, planes, blocks1, got1, absorbed,
    q_product, mixed, wide, leaf_sem, own_sem, a_send, a_recv, r_send, r_recv,
):
    chunks, _, span, columns = part.shape
    width = n * span
    steps = n.bit_length() - 1
    group = n // 4
    me = lax.axis_index("outer")
    lefts, rights = (l0, l1, l2, l3), (r0, r1, r2, r3)

    def flipped(k):
        total = 0
        for s in range(steps):
            both = lax.rem(me // (1 << s), 2) + lax.rem(k // (1 << s), 2)
            total = total + lax.rem(both, 2) * (1 << s)
        return total

    def reversed_bits(k):
        return sum(lax.rem(k // (1 << s), 2) * (n >> (s + 1)) for s in range(steps))

    bit = [lax.rem(me // (1 << s), 2) for s in range(steps)]
    partners = [me + (1 << s) * (1 - 2 * bit[s]) for s in range(steps)]
    starts = [0]
    gives = []
    for s in range(steps):
        half = n >> (s + 1)
        gives.append(starts[s] + (1 - bit[s]) * half)
        starts.append(starts[s] + bit[s] * half)

    barrier = pltpu.get_barrier_semaphore()

    def greet(k, carry):
        pl.semaphore_signal(barrier, inc=1, device_id={"outer": lax.rem(me + k, n)}, device_id_type=MESH)
        return carry

    lax.fori_loop(1, n, greet, 0)

    def leaf_copies(j):
        return (
            pltpu.make_async_copy(left.at[j], lefts[j], leaf_sem.at[j, 0]),
            pltpu.make_async_copy(right.at[j], rights[j], leaf_sem.at[j, 1]),
        )

    def each(first, last, act):
        def one(k, carry):
            act(k)
            return carry

        if last - first <= 4:
            for k in range(first, last):
                act(k)
        else:
            lax.fori_loop(first, last, one, 0)

    def first_copy(k):
        to = flipped(k)
        return pltpu.make_async_remote_copy(
            src_ref=stem.at[to], dst_ref=got0.at[me], send_sem=a_send.at[0, k], recv_sem=a_recv.at[0, k],
            device_id={"outer": to}, device_id_type=MESH)

    def first_arrival(k):
        origin = flipped(k)
        return pltpu.make_async_remote_copy(
            src_ref=stem.at[origin], dst_ref=got0.at[origin], send_sem=a_send.at[0, k], recv_sem=a_recv.at[0, k],
            device_id={"outer": origin}, device_id_type=MESH)

    def second_copy(k):
        to = flipped(k)
        return pltpu.make_async_remote_copy(
            src_ref=blocks1.at[reversed_bits(to)], dst_ref=got1.at[me // 4, lax.rem(me, 4)],
            send_sem=a_send.at[1, k], recv_sem=a_recv.at[1, k],
            device_id={"outer": to}, device_id_type=MESH)

    def second_arrival(k):
        origin = flipped(k)
        return pltpu.make_async_remote_copy(
            src_ref=blocks1.at[reversed_bits(origin)], dst_ref=got1.at[origin // 4, lax.rem(origin, 4)],
            send_sem=a_send.at[1, k], recv_sem=a_recv.at[1, k],
            device_id={"outer": origin}, device_id_type=MESH)

    own_copy = pltpu.make_async_copy(stem.at[me], got0.at[me], own_sem)

    def send_first(i):
        each(group * i if i else 1, group * (i + 1), lambda k: first_copy(k).start())

    def split(i):
        each(group * i if i else 1, group * (i + 1), lambda k: first_arrival(k).wait_recv())
        if i == 0:
            own_copy.wait()
        here = pl.ds(flipped(group * i) // group * group, group)
        rows = group * span
        entries = got0[here].reshape(2 * rows, columns).astype(jnp.float32)
        for t in range(columns // LANES):
            lanes = slice(t * LANES, (t + 1) * LANES)
            wide[t, 0 : 2 * rows] = entries[:, lanes]
            for p in range(2):
                plane = wide[t, pl.ds(p, rows, stride=2), :]
                planes[p, here, :, lanes] = plane.astype(jnp.bfloat16).reshape(group, span, LANES)

    def dot(a, b):
        return jnp.dot(a, b, preferred_element_type=jnp.float32)

    def leaf_product(j):
        for copy in leaf_copies(j):
            copy.wait()
        chosen = bits[j]
        plain_ref, other_ref = (rights[j], lefts[j]) if j % 2 == 0 else (lefts[j], rights[j])
        rows = 2 * plain_ref.shape[1]
        plain = plain_ref[chosen].reshape(rows, plain_ref.shape[3])
        other = other_ref[chosen].reshape(rows, other_ref.shape[3]).astype(jnp.float32)
        even = lax.rem(lax.broadcasted_iota(jnp.int32, other.shape, 0), 2) == 0
        signed = jnp.where(even, other, -other).astype(jnp.bfloat16)
        swapped = jnp.where(even, pltpu.roll(other, rows - 1, 0), pltpu.roll(other, 1, 0)).astype(jnp.bfloat16)
        dims = (((0,), (0,)), ((), ()))
        for p, factor in enumerate((signed, swapped)):
            product = lax.dot_general(plain, factor, dims, preferred_element_type=jnp.float32)
            product = product.reshape(n, span, columns)
            if j == 0:
                for b in range(n):
                    at = sum((b >> s & 1) * (n >> (s + 1)) for s in range(steps))
                    part[p, at] = product[b]
            else:
                part[2 * j + p] = product

    def reduce_copy(c, s):
        half, at = n >> (s + 1), n - (n >> s)
        return pltpu.make_async_remote_copy(
            src_ref=outgoing.at[c, pl.ds(gives[s], half)], dst_ref=incoming.at[c, pl.ds(at, half)],
            send_sem=r_send.at[c, s], recv_sem=r_recv.at[c, s],
            device_id={"outer": partners[s]}, device_id_type=MESH)

    def gather_copy(c, s, first):
        here = branch.at[c, pl.ds(first, n >> (s + 1))]
        return pltpu.make_async_remote_copy(
            src_ref=here, dst_ref=here, send_sem=r_send.at[c, 2 * steps - 1 - s], recv_sem=r_recv.at[c, 2 * steps - 1 - s],
            device_id={"outer": partners[s]}, device_id_type=MESH)

    def begin(c, step):
        if step < steps:
            give = pl.ds(gives[step], n >> (step + 1))
            outgoing[c, give] = part[c, give].astype(outgoing.dtype)
            reduce_copy(c, step).start()
        else:
            s = 2 * steps - 1 - step
            gather_copy(c, s, starts[s + 1]).start()

    def finish(c, step):
        if step < steps:
            half, at = n >> (step + 1), n - (n >> step)
            reduce_copy(c, step).wait_recv()
            keep = pl.ds(starts[step + 1], half)
            total = part[c, keep] + incoming[c, pl.ds(at, half)].astype(jnp.float32)
            if step == steps - 1:
                branch[c, keep] = total.astype(branch.dtype)
            else:
                part[c, keep] = total
        else:
            s = 2 * steps - 1 - step
            gather_copy(c, s, gives[s]).wait_recv()

    def turn(c, step):
        if step:
            finish(c, step - 1)
        if step < 2 * steps:
            begin(c, step)

    def near(low):
        core = lax.rem(bit[0] + low % 2, 2)
        side = lax.rem(bit[1] + low // 2, 2)
        return core, side

    def contract_first(low):
        core, side = near(low)
        here = pl.ds(core * (n // 2) + side * (n // 4), group)
        p_real = branch[0, here].reshape(group * span, width)
        p_imag = branch[1, here].reshape(group * span, width)
        a_real, a_imag = planes[0].reshape(width, columns), planes[1].reshape(width, columns)
        real_part = (dot(p_real, a_real) - dot(p_imag, a_imag)).astype(jnp.bfloat16)
        imag_part = (dot(p_real, a_imag) + dot(p_imag, a_real)).astype(jnp.bfloat16)
        blocks1[here, 0:span] = real_part.reshape(group, span, columns)
        blocks1[here, span : 2 * span] = imag_part.reshape(group, span, columns)
        if low == 0:
            got1[me // 4, lax.rem(me, 4)] = blocks1[starts[steps]]
        if group == 4:
            for q in (2, 3, 1, 0):
                if q or low:
                    second_copy(4 * q + low).start()
        else:
            each(0 if low else 1, group, lambda q: second_copy(4 * q + low).start())

    def interleave():
        for t in range(width // LANES):
            lanes = slice(t * LANES, (t + 1) * LANES)
            p_real, p_imag = (
                branch[4 + p, :, :, lanes].reshape(width, LANES).astype(jnp.float32) for p in range(2))
            for k, (even, odd) in enumerate(((p_real, p_imag), (-p_imag, p_real))):
                wide[t, pl.ds(0, width, stride=2), :] = even
                wide[t, pl.ds(1, width, stride=2), :] = odd
                mixed[k, :, lanes] = wide[t].astype(jnp.bfloat16)

    def multiply():
        a_real, a_imag, b_real, b_imag = (branch[c].reshape(width, columns) for c in (2, 3, 6, 7))
        q_product[0] = (dot(a_real, b_real) - dot(a_imag, b_imag)).astype(jnp.bfloat16)
        q_product[1] = (dot(a_real, b_imag) + dot(a_imag, b_real)).astype(jnp.bfloat16)

    def absorb(low):
        each(0 if low else 1, group, lambda q: second_arrival(4 * q + low).wait_recv())
        core, side = near(low)
        entries = got1[:, core + 2 * side].reshape(group * 2 * span, columns)
        by_real = dot(entries, q_product[0]).reshape(group, 2, span, columns)
        by_imag = dot(entries, q_product[1]).reshape(group, 2, span, columns)
        absorbed[0, :, core + 2 * side] = (by_real[:, 0] - by_imag[:, 1]).astype(absorbed.dtype)
        absorbed[1, :, core + 2 * side] = (by_imag[:, 0] + by_real[:, 1]).astype(absorbed.dtype)

    def contract_last(tile):
        rows = width // 4
        here = pl.ds(2 * rows * tile, 2 * rows)
        a_real, a_imag = absorbed[0].reshape(width, columns), absorbed[1].reshape(width, columns)
        total = dot(mixed[0, here], a_real) + dot(mixed[1, here], a_imag)
        out[rows * tile : rows * (tile + 1)] = total.astype(jnp.bfloat16).reshape(rows, 2, columns)

    for j in (0, 2, 1, 3):
        for copy in leaf_copies(j):
            copy.start()
    own_copy.start()
    pl.semaphore_wait(barrier, n - 1)

    events = []
    for i, time in zip((2, 3, 1, 0), FIRST_SENDS):
        events.append((time, functools.partial(send_first, i)))
    for i, time in zip((2, 3, 1, 0), SPLITS):
        events.append((time, functools.partial(split, i)))
    for j, time in LEAVES.items():
        events.append((time, functools.partial(leaf_product, j)))
    stages = [STAGES[min(s, 3)] for s in range(steps)]
    stages = stages + stages[::-1]
    done = {}
    for j, time in ENTRIES.items():
        for p in range(2):
            for step in range(2 * steps + 1):
                at = time + PLANE_GAP * p + sum(stages[:step])
                events.append((at, functools.partial(turn, 2 * j + p, step)))
                done[j, step] = at
    for low, s in ((0, 2), (2, 1), (1, 0), (3, 0)):
        at = done[0, 2 * steps - s] + 0.01
        assert at > max(SPLITS)
        events.append((at, functools.partial(contract_first, low)))
    end = done[2, 2 * steps] + 0.01
    events.append((end, interleave))
    end = max(done[1, 2 * steps], done[3, 2 * steps]) + 0.01
    events.append((end, multiply))
    end = max(at for at, _ in events)
    for i, low in enumerate((0, 2, 1, 3)):
        events.append((end + i + 1, functools.partial(absorb, low)))
    for tile in range(4):
        events.append((end + tile + 6, functools.partial(contract_last, tile)))
    for _, act in sorted(events, key=lambda event: event[0]):
        act()

    def settle(k, carry):
        first_copy(k).wait_send()
        second_copy(k).wait_send()
        return carry

    lax.fori_loop(1, n, settle, 0)
    for c in range(chunks):
        for s in range(steps):
            reduce_copy(c, s).wait_send()
            gather_copy(c, s, starts[s + 1]).wait_send()


def on_device(n, stem_tensor, leaf_left, leaf_right, slice_bits):
    branches, slices, depth, _, rows = leaf_left.shape
    width, columns = stem_tensor.shape[1], stem_tensor.shape[3]
    span = width // n
    steps = n.bit_length() - 1
    blocks = stem_tensor.reshape(n, span, 2, columns)
    both = (2 * branches, n, span, columns)
    anywhere = pl.BlockSpec(memory_space=pl.ANY)
    state = pl.pallas_call(
        functools.partial(network_kernel, n),
        out_shape=jax.ShapeDtypeStruct((width, 2, columns), jnp.bfloat16),
        in_specs=[pl.BlockSpec(memory_space=pltpu.SMEM), anywhere, anywhere, anywhere],
        out_specs=pl.BlockSpec(memory_space=pltpu.VMEM),
        scratch_shapes=[
            *[pltpu.VMEM((slices, depth, 2, rows), jnp.bfloat16)] * branches,
            *[pltpu.VMEM((slices, depth, 2, columns), jnp.bfloat16)] * branches,
            pltpu.VMEM(both, jnp.float32),
            pltpu.VMEM(both, jnp.bfloat16),
            pltpu.VMEM(both, jnp.bfloat16),
            pltpu.VMEM(both, jnp.bfloat16),
            pltpu.VMEM((n, span, 2, columns), jnp.bfloat16),
            pltpu.VMEM((2, n, span, columns), jnp.bfloat16),
            pltpu.VMEM((n, 2 * span, columns), jnp.bfloat16),
            pltpu.VMEM((n // 4, 4, 2 * span, columns), jnp.bfloat16),
            pltpu.VMEM((2, n // 4, 4, span, columns), jnp.bfloat16),
            pltpu.VMEM((2, width, columns), jnp.bfloat16),
            pltpu.VMEM((2, 2 * width, columns), jnp.bfloat16),
            pltpu.VMEM((columns // LANES, 2 * width, LANES), jnp.float32),
            pltpu.SemaphoreType.DMA((branches, 2)),
            pltpu.SemaphoreType.DMA,
            pltpu.SemaphoreType.DMA((2, n)),
            pltpu.SemaphoreType.DMA((2, n)),
            pltpu.SemaphoreType.DMA((2 * branches, 2 * steps)),
            pltpu.SemaphoreType.DMA((2 * branches, 2 * steps)),
        ],
        compiler_params=pltpu.CompilerParams(
            collective_id=0, has_side_effects=True, vmem_limit_bytes=60 * 1024 * 1024),
    )(slice_bits, blocks, leaf_left, leaf_right)
    return state[None]


def solution(mesh):
    return jax.shard_map(
        functools.partial(on_device, mesh.shape["outer"]),
        mesh=mesh,
        in_specs=(
            P(("cuts", "outer"), None, None, None),
            P(None, None, "outer", None, None),
            P(None, None, "outer", None, None),
            P("cuts"),
        ),
        out_specs=P(("cuts", "outer"), None, None, None),
        check_vma=False,
    )
```

time: 113 us -> 104 us (0.920)
  Pallas kernels: 106 us -> 100 us
  local copies, waits for them, and re-layouts: 5.69 us -> 2.91 us
    pallas_call x2 -> x1, Pallas kernels: 106 us -> 100 us  [on_device(): pl.pallas_call(functools.partial(network_kernel, n), out_shape=jax.ShapeD...]
    reshape x2 -> x0, local copies, waits for them, and re-layouts: 5.69 us -> none  [the longest x1 3.27 us: on_device(): state = contract_network(n, part, blocks).reshape(2, width, columns)]
    unnamed x0 -> x1, local copies, waits for them, and re-layouts: none -> 2.91 us
where the time goes in v1:
time: 104 us; the launch traced here: 103 us
  Pallas kernels  100 us (96%)
  local copies, waits for them, and re-layouts  2.91 us (3%)
    pallas_call x1, Pallas kernels, on_device(): pl.pallas_call(functools.partial(network_kernel, n), out_shape=jax.ShapeD...  100 us
    unnamed x1, local copies, waits for them, and re-layouts  2.91 us

profile of v1, /device:TPU:1, one launch (start us, length us, event | category | flops | bytes accessed | tf_op | source)
XLA Modules:
  0.0 103.1 jit_solution(2535874234809067368)
XLA Ops:
  0.0 100.1 %shard_map.46 = bf16[512,2,512]{2,1,0:T(2,128)(2,1)} custom-call(s32[4]{0:T(128)} %bits.1, bf16[16,32,2,512]{3,2,1,0:T(2,128)(2,1)} %bitcast.3, bf16[4,2,512,2,512]{4,3,2,1,0:T(2,128)(2,1)} %left.1, bf16[4,2,512,2,512]{4,3,2,1,0:T(2,128)(2,1)} %right.1), custom_call_target="tpu_custom_call" | custom-call | tf_op jit(solution)/shard_map/pallas_call | solution.py:301
  100.2 2.9 %copy.6 = bf16[1,512,2,512]{3,2,1,0:T(2,128)(2,1)} copy(bf16[1,512,2,512]{3,2,1,0:T(2,128)(2,1)} %bitcast.2) | data formatting | bytes 2097152

commit v2 on v1

v2 whole, which is shorter than its diff:
```python
import functools

import jax
import jax.numpy as jnp
from jax import lax
from jax.experimental import pallas as pl
from jax.experimental.pallas import tpu as pltpu
from jax.sharding import PartitionSpec as P

MESH = pl.DeviceIdType.MESH
LANES = 128
TILES = 4
LEAF_ORDER = (2, 3, 1)
PIECES = (2, 1, 2, 1)


def pieces_of(planes, span):
    parts = []
    for plane in range(planes):
        pieces = PIECES[plane // 2] if span % 32 == 0 else 1
        parts += [(plane, pl.ds(h * (span // pieces), span // pieces)) for h in range(pieces)]
    return parts


def schedule(n, steps, parts):
    events = []

    def at(time, *event):
        events.append((time, event))

    TABLE = [
        ('first', 14),
        ('first', 3),
        ('turn', 1, 0),
        ('first', 12),
        ('first', 4),
        ('first', 9),
        ('turn', 3, 0),
        ('first', 2),
        ('leaf', 2),
        ('first', 5),
        ('turn', 6, 0),
        ('turn', 7, 0),
        ('turn', 3, 1),
        ('leaf', 3),
        ('turn', 1, 1),
        ('turn', 0, 0),
        ('turn', 7, 1),
        ('turn', 11, 0),
        ('turn', 2, 0),
        ('leaf', 1),
        ('first', 1),
        ('turn', 3, 2),
        ('turn', 0, 1),
        ('turn', 9, 0),
        ('turn', 1, 2),
        ('turn', 10, 0),
        ('turn', 2, 1),
        ('turn', 4, 0),
        ('turn', 11, 1),
        ('turn', 6, 1),
        ('turn', 8, 0),
        ('first', 13),
        ('turn', 3, 3),
        ('turn', 7, 2),
        ('first', 8),
        ('first', 15),
        ('turn', 5, 0),
        ('turn', 8, 1),
        ('turn', 0, 2),
        ('turn', 5, 1),
        ('turn', 2, 2),
        ('turn', 3, 4),
        ('turn', 11, 2),
        ('turn', 7, 3),
        ('turn', 1, 3),
        ('turn', 10, 1),
        ('turn', 0, 3),
        ('turn', 2, 3),
        ('turn', 9, 1),
        ('first', 6),
        ('turn', 8, 2),
        ('turn', 11, 3),
        ('turn', 6, 2),
        ('split', 0),
        ('turn', 7, 4),
        ('turn', 5, 2),
        ('split', 3),
        ('turn', 2, 4),
        ('first', 7),
        ('turn', 3, 5),
        ('first', 11),
        ('turn', 0, 4),
        ('turn', 10, 2),
        ('turn', 4, 1),
        ('turn', 8, 3),
        ('turn', 1, 4),
        ('turn', 5, 3),
        ('first', 10),
        ('turn', 11, 4),
        ('turn', 2, 5),
        ('turn', 3, 6),
        ('turn', 4, 2),
        ('turn', 0, 5),
        ('turn', 1, 5),
        ('split', 1),
        ('turn', 8, 4),
        ('turn', 3, 7),
        ('turn', 7, 5),
        ('turn', 9, 2),
        ('turn', 2, 6),
        ('turn', 6, 3),
        ('turn', 5, 4),
        ('turn', 4, 3),
        ('turn', 10, 3),
        ('split', 2),
        ('turn', 1, 6),
        ('turn', 11, 5),
        ('turn', 7, 6),
        ('turn', 0, 6),
        ('turn', 8, 5),
        ('turn', 3, 8),
        ('turn', 2, 7),
        ('contract', 0),
        ('turn', 6, 4),
        ('turn', 9, 3),
        ('turn', 5, 5),
        ('turn', 4, 4),
        ('turn', 11, 6),
        ('turn', 10, 4),
        ('turn', 1, 7),
        ('turn', 0, 7),
        ('second', 12),
        ('turn', 6, 5),
        ('contract', 2),
        ('turn', 8, 6),
        ('turn', 4, 5),
        ('turn', 5, 6),
        ('second', 10),
        ('turn', 11, 7),
        ('turn', 9, 4),
        ('second', 14),
        ('turn', 0, 8),
        ('turn', 8, 7),
        ('turn', 10, 5),
        ('turn', 4, 6),
        ('turn', 1, 8),
        ('turn', 2, 8),
        ('second', 8),
        ('contract', 1),
        ('turn', 6, 6),
        ('second', 5),
        ('second', 9),
        ('turn', 10, 6),
        ('turn', 9, 5),
        ('turn', 4, 7),
        ('second', 6),
        ('turn', 8, 8),
        ('turn', 5, 7),
        ('second', 13),
        ('turn', 9, 6),
        ('contract', 3),
        ('second', 15),
        ('turn', 10, 7),
        ('turn', 6, 7),
        ('second', 4),
        ('second', 2),
        ('turn', 7, 7),
        ('turn', 11, 8),
        ('turn', 5, 8),
        ('second', 11),
        ('second', 3),
        ('turn', 6, 8),
        ('turn', 10, 8),
        ('turn', 9, 7),
        ('turn', 4, 8),
        ('multiply',),
        ('second', 7),
        ('turn', 7, 8),
        ('second', 1),
        ('absorb', 1),
        ('absorb', 0),
        ('absorb', 2),
        ('turn', 9, 8),
        ('interleave',),
        ('absorb', 3),
    ]
    if n == 16:
        return TABLE
    return [event for _, event in sorted(events, key=lambda entry: entry[0])]


def network_kernel(
    n, bits, stem, left, right, mixed_out, absorbed_out,
    l0, l1, l2, l3, r0, r1, r2, r3, part, outgoing, incoming, branch, got0, planes, blocks1, got1, absorbed,
    q_product, mixed, wide, leaf_sem, own_sem, a_send, a_recv, r_send, r_recv,
):
    planes_in, _, span, columns = part.shape
    parts = pieces_of(planes_in, span)
    chunks = len(parts)
    width = n * span
    steps = n.bit_length() - 1
    group = n // 4
    me = lax.axis_index("outer")
    lefts, rights = (l0, l1, l2, l3), (r0, r1, r2, r3)

    bit = [lax.rem(me // (1 << s), 2) for s in range(steps)]

    def flipped(k):
        return sum((1 - bit[s] if k >> s & 1 else bit[s]) * (1 << s) for s in range(steps))

    def reversed_bits(k):
        return sum(lax.rem(k // (1 << s), 2) * (n >> (s + 1)) for s in range(steps))

    partners = [me + (1 << s) * (1 - 2 * bit[s]) for s in range(steps)]
    starts = [0]
    gives = []
    for s in range(steps):
        half = n >> (s + 1)
        gives.append(starts[s] + (1 - bit[s]) * half)
        starts.append(starts[s] + bit[s] * half)

    barrier = pltpu.get_barrier_semaphore()

    def greet(k, carry):
        pl.semaphore_signal(barrier, inc=1, device_id={"outer": lax.rem(me + k, n)}, device_id_type=MESH)
        return carry

    lax.fori_loop(1, n, greet, 0)

    def leaf_copies(j):
        return (
            pltpu.make_async_copy(left.at[j], lefts[j], leaf_sem.at[j, 0]),
            pltpu.make_async_copy(right.at[j], rights[j], leaf_sem.at[j, 1]),
        )

    def first_copy(k):
        to = flipped(k)
        return pltpu.make_async_remote_copy(
            src_ref=stem.at[to], dst_ref=got0.at[me], send_sem=a_send.at[k], recv_sem=a_recv.at[0, k // group],
            device_id={"outer": to}, device_id_type=MESH)

    def second_copy(k):
        to = flipped(k)
        return pltpu.make_async_remote_copy(
            src_ref=blocks1.at[reversed_bits(to)], dst_ref=got1.at[me // 4, lax.rem(me, 4)],
            send_sem=a_send.at[k], recv_sem=a_recv.at[1, k % 4],
            device_id={"outer": to}, device_id_type=MESH)

    own_copy = pltpu.make_async_copy(stem.at[me], got0.at[me], a_recv.at[0, 0])

    unsettled = {}

    def launch(copy, *slot):
        if slot in unsettled:
            unsettled[slot].wait_send()
        copy.start()
        unsettled[slot] = copy

    def send_first(k):
        launch(first_copy(k), k)

    def send_second(k):
        launch(second_copy(k), k)

    def split(i):
        here = pl.ds(flipped(group * i) // group * group, group)
        pltpu.make_async_copy(got0.at[here], got0.at[here], a_recv.at[0, i]).wait()
        rows = group * span
        entries = got0[here].reshape(2 * rows, columns).astype(jnp.float32)
        for t in range(columns // LANES):
            lanes = slice(t * LANES, (t + 1) * LANES)
            wide[t, 0 : 2 * rows] = entries[:, lanes]
            for p in range(2):
                plane = wide[t, pl.ds(p, rows, stride=2), :]
                planes[p, here, :, lanes] = plane.astype(jnp.bfloat16).reshape(group, span, LANES)

    def dot(a, b):
        return jnp.dot(a, b, preferred_element_type=jnp.float32)

    def leaf_product(j):
        for copy in leaf_copies(j):
            copy.wait()
        chosen = bits[j]
        plain_ref, other_ref = (rights[j], lefts[j]) if j % 2 == 0 else (lefts[j], rights[j])
        rows = 2 * plain_ref.shape[1]
        plain = plain_ref[chosen].reshape(rows, plain_ref.shape[3])
        other = other_ref[chosen].reshape(rows, other_ref.shape[3]).astype(jnp.float32)
        even = lax.rem(lax.broadcasted_iota(jnp.int32, other.shape, 0), 2) == 0
        signed = jnp.where(even, other, -other).astype(jnp.bfloat16)
        swapped = jnp.where(even, pltpu.roll(other, rows - 1, 0), pltpu.roll(other, 1, 0)).astype(jnp.bfloat16)
        dims = (((0,), (0,)), ((), ()))
        for p, factor in enumerate((signed, swapped)):
            product = lax.dot_general(plain, factor, dims, preferred_element_type=jnp.float32)
            product = product.reshape(n, span, columns)
            if j == 0:
                for b in range(n):
                    at = sum((b >> s & 1) * (n >> (s + 1)) for s in range(steps))
                    part[p, at] = product[b]
            else:
                part[2 * j + p] = product

    def reduce_copy(c, s):
        half, at = n >> (s + 1), n - (n >> s)
        plane, rows = parts[c]
        return pltpu.make_async_remote_copy(
            src_ref=outgoing.at[plane, pl.ds(gives[s], half), rows], dst_ref=incoming.at[plane, pl.ds(at, half), rows],
            send_sem=r_send.at[c], recv_sem=r_recv.at[c, s],
            device_id={"outer": partners[s]}, device_id_type=MESH)

    def gather_copy(c, s, first):
        plane, rows = parts[c]
        here = branch.at[plane, pl.ds(first, n >> (s + 1)), rows]
        return pltpu.make_async_remote_copy(
            src_ref=here, dst_ref=here, send_sem=r_send.at[c], recv_sem=r_recv.at[c, 2 * steps - 1 - s],
            device_id={"outer": partners[s]}, device_id_type=MESH)

    def begin(c, step):
        if step < steps:
            plane, rows = parts[c]
            give = pl.ds(gives[step], n >> (step + 1))
            outgoing[plane, give, rows] = part[plane, give, rows].astype(outgoing.dtype)
            launch(reduce_copy(c, step), 'chunk', c)
        else:
            s = 2 * steps - 1 - step
            launch(gather_copy(c, s, starts[s + 1]), 'chunk', c)

    def finish(c, step):
        if step < steps:
            plane, rows = parts[c]
            half, at = n >> (step + 1), n - (n >> step)
            reduce_copy(c, step).wait_recv()
            keep = pl.ds(starts[step + 1], half)
            total = part[plane, keep, rows] + incoming[plane, pl.ds(at, half), rows].astype(jnp.float32)
            if step == steps - 1:
                branch[plane, keep, rows] = total.astype(branch.dtype)
            else:
                part[plane, keep, rows] = total
        else:
            s = 2 * steps - 1 - step
            gather_copy(c, s, gives[s]).wait_recv()

    def turn(c, step):
        if step:
            finish(c, step - 1)
        if step < 2 * steps:
            begin(c, step)

    def near(low):
        core = lax.rem(bit[0] + low % 2, 2)
        side = lax.rem(bit[1] + low // 2, 2)
        return core, side

    def contract_first(low):
        core, side = near(low)
        here = pl.ds(core * (n // 2) + side * (n // 4), group)
        p_real = branch[0, here].reshape(group * span, width)
        p_imag = branch[1, here].reshape(group * span, width)
        a_real, a_imag = planes[0].reshape(width, columns), planes[1].reshape(width, columns)
        real_part = (dot(p_real, a_real) - dot(p_imag, a_imag)).astype(jnp.bfloat16)
        imag_part = (dot(p_real, a_imag) + dot(p_imag, a_real)).astype(jnp.bfloat16)
        blocks1[here, 0:span] = real_part.reshape(group, span, columns)
        blocks1[here, span : 2 * span] = imag_part.reshape(group, span, columns)
        if low == 0:
            got1[me // 4, lax.rem(me, 4)] = blocks1[starts[steps]]

    stored = []

    def put(source, target, semaphore):
        copy = pltpu.make_async_copy(source, target, semaphore)
        copy.start()
        stored.append(copy)

    def interleave():
        for t in range(width // LANES):
            lanes = slice(t * LANES, (t + 1) * LANES)
            p_real, p_imag = (
                branch[4 + p, :, :, lanes].reshape(width, LANES).astype(jnp.float32) for p in range(2))
            for k, (even, odd) in enumerate(((p_real, p_imag), (-p_imag, p_real))):
                wide[t, pl.ds(0, width, stride=2), :] = even
                wide[t, pl.ds(1, width, stride=2), :] = odd
                mixed[k, :, lanes] = wide[t].astype(jnp.bfloat16)
        put(mixed, mixed_out, own_sem)

    def multiply():
        a_real, a_imag, b_real, b_imag = (branch[c].reshape(width, columns) for c in (2, 3, 6, 7))
        q_product[0] = (dot(a_real, b_real) - dot(a_imag, b_imag)).astype(jnp.bfloat16)
        q_product[1] = (dot(a_real, b_imag) + dot(a_imag, b_real)).astype(jnp.bfloat16)

    def absorb(low):
        fill = got1.at[pl.ds(0, group if low else group - 1), 0]
        pltpu.make_async_copy(fill, fill, a_recv.at[1, low]).wait()
        core, side = near(low)
        entries = got1[:, core + 2 * side].reshape(group * 2 * span, columns)
        by_real = dot(entries, q_product[0]).reshape(group, 2, span, columns)
        by_imag = dot(entries, q_product[1]).reshape(group, 2, span, columns)
        absorbed[0, :, core + 2 * side] = (by_real[:, 0] - by_imag[:, 1]).astype(absorbed.dtype)
        absorbed[1, :, core + 2 * side] = (by_imag[:, 0] + by_real[:, 1]).astype(absorbed.dtype)
        for p in range(2):
            put(absorbed.at[p, :, core + 2 * side], absorbed_out.at[p, :, core + 2 * side], leaf_sem.at[low, p])

    for copy in leaf_copies(0):
        copy.start()
    own_copy.start()
    leaf_product(0)
    for j in LEAF_ORDER:
        for copy in leaf_copies(j):
            copy.start()
    pl.semaphore_wait(barrier, n - 1)

    acts = dict(
        leaf=leaf_product, turn=turn, first=send_first, split=split, contract=contract_first, second=send_second,
        interleave=interleave, multiply=multiply, absorb=absorb)
    for name, *arguments in schedule(n, steps, parts):
        acts[name](*arguments)

    for copy in unsettled.values():
        copy.wait_send()
    for copy in stored:
        copy.wait()


def last_kernel(mixed, absorbed, out, mixed_here, absorbed_here, out_here, semaphores):
    rows = mixed.shape[1] // TILES
    copies = []
    for tile in range(TILES):
        here = pl.ds(tile * rows, rows)
        copies.append(pltpu.make_async_copy(mixed.at[:, here], mixed_here.at[:, here], semaphores.at[tile]))
    fetch = pltpu.make_async_copy(absorbed, absorbed_here, semaphores.at[TILES])
    copies[0].start()
    fetch.start()
    for copy in copies[1:]:
        copy.start()
    stores = []
    for tile, copy in enumerate(copies):
        copy.wait()
        if tile == 0:
            fetch.wait()
        here = pl.ds(tile * rows, rows)
        half = pl.ds(tile * (rows // 2), rows // 2)
        total = jnp.dot(mixed_here[0, here], absorbed_here[0], preferred_element_type=jnp.float32)
        total = total + jnp.dot(mixed_here[1, here], absorbed_here[1], preferred_element_type=jnp.float32)
        out_here[half] = total.astype(out.dtype).reshape(rows // 2, 2, out.shape[2])
        stores.append(pltpu.make_async_copy(out_here.at[half], out.at[half], semaphores.at[tile]))
        stores[-1].start()
    for store in stores:
        store.wait()


def contract_last(mixed, absorbed):
    _, rows, width = mixed.shape
    columns = absorbed.shape[2]
    anywhere = pl.BlockSpec(memory_space=pl.ANY)
    return pl.pallas_call(
        last_kernel,
        out_shape=jax.ShapeDtypeStruct((rows // 2, 2, columns), jnp.bfloat16),
        in_specs=[anywhere, anywhere],
        out_specs=anywhere,
        scratch_shapes=[
            pltpu.VMEM(mixed.shape, mixed.dtype),
            pltpu.VMEM(absorbed.shape, absorbed.dtype),
            pltpu.VMEM((rows // 2, 2, columns), jnp.bfloat16),
            pltpu.SemaphoreType.DMA((TILES + 1,)),
        ],
    )(mixed, absorbed)


def on_device(n, stem_tensor, leaf_left, leaf_right, slice_bits):
    branches, slices, depth, _, rows = leaf_left.shape
    width, columns = stem_tensor.shape[1], stem_tensor.shape[3]
    span = width // n
    steps = n.bit_length() - 1
    chunks = len(pieces_of(2 * branches, span))
    blocks = stem_tensor.reshape(n, span, 2, columns)
    both = (2 * branches, n, span, columns)
    anywhere = pl.BlockSpec(memory_space=pl.ANY)
    mixed, absorbed = pl.pallas_call(
        functools.partial(network_kernel, n),
        out_shape=(
            jax.ShapeDtypeStruct((2, 2 * width, width), jnp.bfloat16),
            jax.ShapeDtypeStruct((2, n // 4, 4, span, columns), jnp.bfloat16),
        ),
        in_specs=[pl.BlockSpec(memory_space=pltpu.SMEM), anywhere, anywhere, anywhere],
        out_specs=(anywhere, anywhere),
        scratch_shapes=[
            *[pltpu.VMEM((slices, depth, 2, rows), jnp.bfloat16)] * branches,
            *[pltpu.VMEM((slices, depth, 2, columns), jnp.bfloat16)] * branches,
            pltpu.VMEM(both, jnp.float32),
            pltpu.VMEM(both, jnp.bfloat16),
            pltpu.VMEM(both, jnp.bfloat16),
            pltpu.VMEM(both, jnp.bfloat16),
            pltpu.VMEM((n, span, 2, columns), jnp.bfloat16),
            pltpu.VMEM((2, n, span, columns), jnp.bfloat16),
            pltpu.VMEM((n, 2 * span, columns), jnp.bfloat16),
            pltpu.VMEM((n // 4, 4, 2 * span, columns), jnp.bfloat16),
            pltpu.VMEM((2, n // 4, 4, span, columns), jnp.bfloat16),
            pltpu.VMEM((2, width, columns), jnp.bfloat16),
            pltpu.VMEM((2, 2 * width, columns), jnp.bfloat16),
            pltpu.VMEM((columns // LANES, 2 * width, LANES), jnp.float32),
            pltpu.SemaphoreType.DMA((branches, 2)),
            pltpu.SemaphoreType.DMA,
            pltpu.SemaphoreType.DMA((n,)),
            pltpu.SemaphoreType.DMA((2, 4)),
            pltpu.SemaphoreType.DMA((chunks,)),
            pltpu.SemaphoreType.DMA((chunks, 2 * steps)),
        ],
        compiler_params=pltpu.CompilerParams(
            collective_id=0, has_side_effects=True, vmem_limit_bytes=60 * 1024 * 1024),
    )(slice_bits, blocks, leaf_left, leaf_right)
    return contract_last(mixed, absorbed.reshape(2, width, columns))[None]


def solution(mesh):
    return jax.shard_map(
        functools.partial(on_device, mesh.shape["outer"]),
        mesh=mesh,
        in_specs=(
            P(("cuts", "outer"), None, None, None),
            P(None, None, "outer", None, None),
            P(None, None, "outer", None, None),
            P("cuts"),
        ),
        out_specs=P(("cuts", "outer"), None, None, None),
        check_vma=False,
    )
```

time: 104 us -> 91.2 us (0.88)
  Pallas kernels: 100 us -> 90.9 us
  local copies, waits for them, and re-layouts: 2.91 us -> 0 us
    pallas_call x1 -> x2, Pallas kernels: 100 us -> 90.9 us  [the longest x1 86.9 us: on_device(): pl.pallas_call(functools.partial(network_kernel, n), out_shape=(jax.Shape...]
    unnamed x1 -> x0, local copies, waits for them, and re-layouts: 2.91 us -> none
where the time goes in v2:
time: 91.2 us; the launch traced here: 91 us
  Pallas kernels  90.9 us (100%)
    pallas_call x1, Pallas kernels, on_device(): pl.pallas_call(functools.partial(network_kernel, n), out_shape=(jax.Shape...  86.9 us
    pallas_call x1, Pallas kernels, contract_last(): pl.pallas_call(last_kernel, out_shape=jax.ShapeDtypeStruct((rows // 2, 2,...  3.91 us

profile of v2, /device:TPU:1, one launch (start us, length us, event | category | flops | bytes accessed | tf_op | source)
XLA Modules:
  0.0 91.0 jit_solution(4538142757654786965)
XLA Ops:
  0.0 86.9 %shard_map.46 = (bf16[2,1024,512]{2,1,0:T(8,128)(2,1)}, bf16[2,4,4,32,512]{4,3,2,1,0:T(8,128)(2,1)}) custom-call(s32[4]{0:T(128)} %bits.1, bf16[16,32,2,512]{3,2,1,0:T(2,128)(2,1)} %bitcast.3, bf16[4,2,512,2,512]{4,3,2,1,0:T(2,128)(2,1)} %left.1, bf16[4,2,512,2,512]{4,3,2,1,0:T(2,128)(2,1)} %right.1), custom_call_target="tpu_custom_call" | custom-call | tf_op jit(solution)/shard_map/pallas_call | solution.py:477
  87.0 3.9 %shard_map.47 = bf16[512,2,512]{2,1,0:T(2,128)(2,1)} custom-call(bf16[2,1024,512]{2,1,0:T(8,128)(2,1)} %get-tuple-element.7.mixed, bf16[2,512,512]{2,1,0:T(8,128)(2,1)} %bitcast.4), custom_call_target="tpu_custom_call" | custom-call | tf_op jit(solution)/shard_map/pallas_call | solution.py:454

commit v3 on v2

--- a/solution.py
+++ b/solution.py
@@ -10,8 +10,171 @@
 MESH = pl.DeviceIdType.MESH
 LANES = 128
 TILES = 4
-LEAF_ORDER = (2, 3, 1)
+HALVES = 1
+LEAF_ORDER = (3, 2, 1)
 PIECES = (2, 1, 2, 1)
+
+
+STAGES = (1.6, 4.5, 3.5, 3.5)
+ENTRIES = (0.5, 15.0, 7.0, 20.0)
+GAP = 0.4
+TABLE = [
+    ('first', 14),
+    ('turn', 0, 0),
+    ('turn', 3, 0),
+    ('leaf', 3),
+    ('turn', 2, 0),
+    ('first', 15),
+    ('turn', 0, 1),
+    ('turn', 1, 0),
+    ('first', 5),
+    ('first', 12),
+    ('first', 4),
+    ('turn', 2, 1),
+    ('leaf', 2),
+    ('turn', 3, 1),
+    ('first', 1),
+    ('turn', 8, 0),
+    ('leaf', 1),
+    ('turn', 1, 1),
+    ('turn', 6, 0),
+    ('turn', 0, 2),
+    ('turn', 8, 1),
+    ('first', 8),
+    ('turn', 4, 0),
+    ('turn', 7, 0),
+    ('turn', 2, 2),
+    ('first', 10),
+    ('turn', 7, 1),
+    ('turn', 0, 3),
+    ('turn', 5, 0),
+    ('turn', 3, 2),
+    ('first', 9),
+    ('turn', 1, 2),
+    ('turn', 11, 0),
+    ('turn', 6, 1),
+    ('turn', 2, 3),
+    ('turn', 4, 1),
+    ('turn', 7, 2),
+    ('turn', 3, 3),
+    ('turn', 10, 0),
+    ('turn', 5, 1),
+    ('turn', 8, 2),
+    ('turn', 0, 4),
+    ('turn', 6, 2),
+    ('turn', 7, 3),
+    ('turn', 1, 3),
+    ('first', 7),
+    ('turn', 9, 0),
+    ('turn', 4, 2),
+    ('turn', 8, 3),
+    ('turn', 0, 5),
+    ('turn', 11, 1),
+    ('turn', 2, 4),
+    ('turn', 1, 4),
+    ('turn', 5, 2),
+    ('turn', 8, 4),
+    ('turn', 3, 4),
+    ('turn', 6, 3),
+    ('turn', 11, 2),
+    ('turn', 9, 1),
+    ('first', 2),
+    ('first', 6),
+    ('turn', 4, 3),
+    ('turn', 5, 3),
+    ('turn', 3, 5),
+    ('turn', 10, 1),
+    ('turn', 6, 4),
+    ('turn', 2, 5),
+    ('first', 13),
+    ('turn', 1, 5),
+    ('turn', 11, 3),
+    ('turn', 9, 2),
+    ('split', 1),
+    ('first', 3),
+    ('turn', 3, 6),
+    ('turn', 6, 5),
+    ('turn', 4, 4),
+    ('turn', 8, 5),
+    ('turn', 2, 6),
+    ('turn', 10, 2),
+    ('turn', 5, 4),
+    ('first', 11),
+    ('turn', 0, 6),
+    ('turn', 4, 5),
+    ('turn', 3, 7),
+    ('turn', 1, 6),
+    ('turn', 9, 3),
+    ('turn', 2, 7),
+    ('turn', 7, 4),
+    ('turn', 8, 6),
+    ('turn', 0, 7),
+    ('turn', 3, 8),
+    ('turn', 10, 3),
+    ('turn', 5, 5),
+    ('turn', 6, 6),
+    ('turn', 9, 4),
+    ('turn', 11, 4),
+    ('split', 0),
+    ('turn', 4, 6),
+    ('turn', 0, 8),
+    ('turn', 1, 7),
+    ('split', 2),
+    ('turn', 2, 8),
+    ('turn', 7, 5),
+    ('split', 3),
+    ('contract', 2),
+    ('turn', 10, 4),
+    ('turn', 1, 8),
+    ('turn', 5, 6),
+    ('second', 14),
+    ('turn', 11, 5),
+    ('second', 10),
+    ('contract', 0),
+    ('contract', 3),
+    ('turn', 10, 5),
+    ('second', 12),
+    ('second', 8),
+    ('turn', 7, 6),
+    ('contract', 1),
+    ('turn', 11, 6),
+    ('turn', 9, 5),
+    ('turn', 10, 6),
+    ('turn', 6, 7),
+    ('turn', 7, 7),
+    ('turn', 8, 7),
+    ('second', 6),
+    ('turn', 9, 6),
+    ('second', 13),
+    ('second', 5),
+    ('turn', 4, 7),
+    ('second', 11),
+    ('turn', 5, 7),
+    ('second', 15),
+    ('turn', 4, 8),
+    ('turn', 8, 8),
+    ('turn', 7, 8),
+    ('second', 4),
+    ('turn', 11, 7),
+    ('turn', 10, 7),
+    ('second', 7),
+    ('second', 1),
+    ('turn', 11, 8),
+    ('second', 2),
+    ('second', 9),
+    ('turn', 9, 7),
+    ('turn', 10, 8),
+    ('second', 3),
+    ('turn', 6, 8),
+    ('turn', 5, 8),
+    ('multiply',),
+    ('turn', 9, 8),
+    ('absorb', 0),
+    ('interleave',),
+    ('absorb', 2),
+    ('absorb', 3),
+    ('absorb', 1),
+]
 
 
 def pieces_of(planes, span):
@@ -23,176 +186,46 @@
 
 
 def schedule(n, steps, parts):
+    if n == 16:
+        return TABLE
     events = []
 
     def at(time, *event):
         events.append((time, event))
 
-    TABLE = [
-        ('first', 14),
-        ('first', 3),
-        ('turn', 1, 0),
-        ('first', 12),
-        ('first', 4),
-        ('first', 9),
-        ('turn', 3, 0),
-        ('first', 2),
-        ('leaf', 2),
-        ('first', 5),
-        ('turn', 6, 0),
-        ('turn', 7, 0),
-        ('turn', 3, 1),
-        ('leaf', 3),
-        ('turn', 1, 1),
-        ('turn', 0, 0),
-        ('turn', 7, 1),
-        ('turn', 11, 0),
-        ('turn', 2, 0),
-        ('leaf', 1),
-        ('first', 1),
-        ('turn', 3, 2),
-        ('turn', 0, 1),
-        ('turn', 9, 0),
-        ('turn', 1, 2),
-        ('turn', 10, 0),
-        ('turn', 2, 1),
-        ('turn', 4, 0),
-        ('turn', 11, 1),
-        ('turn', 6, 1),
-        ('turn', 8, 0),
-        ('first', 13),
-        ('turn', 3, 3),
-        ('turn', 7, 2),
-        ('first', 8),
-        ('first', 15),
-        ('turn', 5, 0),
-        ('turn', 8, 1),
-        ('turn', 0, 2),
-        ('turn', 5, 1),
-        ('turn', 2, 2),
-        ('turn', 3, 4),
-        ('turn', 11, 2),
-        ('turn', 7, 3),
-        ('turn', 1, 3),
-        ('turn', 10, 1),
-        ('turn', 0, 3),
-        ('turn', 2, 3),
-        ('turn', 9, 1),
-        ('first', 6),
-        ('turn', 8, 2),
-        ('turn', 11, 3),
-        ('turn', 6, 2),
-        ('split', 0),
-        ('turn', 7, 4),
-        ('turn', 5, 2),
-        ('split', 3),
-        ('turn', 2, 4),
-        ('first', 7),
-        ('turn', 3, 5),
-        ('first', 11),
-        ('turn', 0, 4),
-        ('turn', 10, 2),
-        ('turn', 4, 1),
-        ('turn', 8, 3),
-        ('turn', 1, 4),
-        ('turn', 5, 3),
-        ('first', 10),
-        ('turn', 11, 4),
-        ('turn', 2, 5),
-        ('turn', 3, 6),
-        ('turn', 4, 2),
-        ('turn', 0, 5),
-        ('turn', 1, 5),
-        ('split', 1),
-        ('turn', 8, 4),
-        ('turn', 3, 7),
-        ('turn', 7, 5),
-        ('turn', 9, 2),
-        ('turn', 2, 6),
-        ('turn', 6, 3),
-        ('turn', 5, 4),
-        ('turn', 4, 3),
-        ('turn', 10, 3),
-        ('split', 2),
-        ('turn', 1, 6),
-        ('turn', 11, 5),
-        ('turn', 7, 6),
-        ('turn', 0, 6),
-        ('turn', 8, 5),
-        ('turn', 3, 8),
-        ('turn', 2, 7),
-        ('contract', 0),
-        ('turn', 6, 4),
-        ('turn', 9, 3),
-        ('turn', 5, 5),
-        ('turn', 4, 4),
-        ('turn', 11, 6),
-        ('turn', 10, 4),
-        ('turn', 1, 7),
-        ('turn', 0, 7),
-        ('second', 12),
-        ('turn', 6, 5),
-        ('contract', 2),
-        ('turn', 8, 6),
-        ('turn', 4, 5),
-        ('turn', 5, 6),
-        ('second', 10),
-        ('turn', 11, 7),
-        ('turn', 9, 4),
-        ('second', 14),
-        ('turn', 0, 8),
-        ('turn', 8, 7),
-        ('turn', 10, 5),
-        ('turn', 4, 6),
-        ('turn', 1, 8),
-        ('turn', 2, 8),
-        ('second', 8),
-        ('contract', 1),
-        ('turn', 6, 6),
-        ('second', 5),
-        ('second', 9),
-        ('turn', 10, 6),
-        ('turn', 9, 5),
-        ('turn', 4, 7),
-        ('second', 6),
-        ('turn', 8, 8),
-        ('turn', 5, 7),
-        ('second', 13),
-        ('turn', 9, 6),
-        ('contract', 3),
-        ('second', 15),
-        ('turn', 10, 7),
-        ('turn', 6, 7),
-        ('second', 4),
-        ('second', 2),
-        ('turn', 7, 7),
-        ('turn', 11, 8),
-        ('turn', 5, 8),
-        ('second', 11),
-        ('second', 3),
-        ('turn', 6, 8),
-        ('turn', 10, 8),
-        ('turn', 9, 7),
-        ('turn', 4, 8),
-        ('multiply',),
-        ('second', 7),
-        ('turn', 7, 8),
-        ('second', 1),
-        ('absorb', 1),
-        ('absorb', 0),
-        ('absorb', 2),
-        ('turn', 9, 8),
-        ('interleave',),
-        ('absorb', 3),
-    ]
-    if n == 16:
-        return TABLE
+    stages = [STAGES[min(s, 3)] for s in range(steps)]
+    stages = stages + stages[::-1]
+    done = {}
+    for c, (plane, _) in enumerate(parts):
+        begin = ENTRIES[plane // 2] + GAP * (plane % 2)
+        for step in range(2 * steps + 1):
+            done[c, step] = begin + sum(stages[:step])
+            at(done[c, step], "turn", c, step)
+    chunks_of = [[c for c, (plane, _) in enumerate(parts) if plane // 2 == j] for j in range(4)]
+    for j in LEAF_ORDER:
+        at(ENTRIES[j] - 1, "leaf", j)
+    ready = max(done[c, 2 * steps - 2] for c in chunks_of[0])
+    for k in range(1, n):
+        at(ready * k / (2 * n), "first", k)
+    for i in range(4):
+        at(ready * (i + 5) / 10, "split", i)
+    for low, s in ((0, 2), (2, 1), (1, 0), (3, 0)):
+        time = max(done[c, 2 * steps - s] for c in chunks_of[0]) + 0.01 * (1 + low)
+        at(time, "contract", low)
+        for q in range(n // 4):
+            if q or low:
+                at(time, "second", 4 * q + low)
+    end = max(done.values()) + 1
+    at(end, "interleave")
+    at(end, "multiply")
+    for i, low in enumerate((0, 2, 1, 3)):
+        at(end + i + 1, "absorb", low)
     return [event for _, event in sorted(events, key=lambda entry: entry[0])]
 
 
 def network_kernel(
-    n, bits, stem, left, right, mixed_out, absorbed_out,
-    l0, l1, l2, l3, r0, r1, r2, r3, part, outgoing, incoming, branch, got0, planes, blocks1, got1, absorbed,
+    n, bits_in, stem, left, right, mixed_out, absorbed_out,
+    bits,    l0, l1, l2, l3, r0, r1, r2, r3, part, outgoing, incoming, branch, got0, planes, blocks1, got1, absorbed,
     q_product, mixed, wide, leaf_sem, own_sem, a_send, a_recv, r_send, r_recv,
 ):
     planes_in, _, span, columns = part.shape
@@ -227,11 +260,16 @@
         return carry
 
     lax.fori_loop(1, n, greet, 0)
-
-    def leaf_copies(j):
+    bits_copy = pltpu.make_async_copy(bits_in, bits, own_sem)
+    bits_copy.start()
+
+    depth = l0.shape[1]
+
+    def leaf_copies(j, piece=0, pieces=1):
+        here = pl.ds(piece * (depth // pieces), depth // pieces)
         return (
-            pltpu.make_async_copy(left.at[j], lefts[j], leaf_sem.at[j, 0]),
-            pltpu.make_async_copy(right.at[j], rights[j], leaf_sem.at[j, 1]),
+            pltpu.make_async_copy(left.at[j, :, here], lefts[j].at[:, here], leaf_sem.at[j + piece, 0]),
+            pltpu.make_async_copy(right.at[j, :, here], rights[j].at[:, here], leaf_sem.at[j + piece, 1]),
         )
 
     def first_copy(k):
@@ -278,14 +316,19 @@
     def dot(a, b):
         return jnp.dot(a, b, preferred_element_type=jnp.float32)
 
-    def leaf_product(j):
-        for copy in leaf_copies(j):
+    def leaf_product(j, piece=0, pieces=1):
+        for copy in leaf_copies(j, piece, pieces):
             copy.wait()
+        if j == 0 and piece == pieces - 1:
+            for other in LEAF_ORDER:
+                for copy in leaf_copies(other):
+                    copy.start()
         chosen = bits[j]
         plain_ref, other_ref = (rights[j], lefts[j]) if j % 2 == 0 else (lefts[j], rights[j])
-        rows = 2 * plain_ref.shape[1]
-        plain = plain_ref[chosen].reshape(rows, plain_ref.shape[3])
-        other = other_ref[chosen].reshape(rows, other_ref.shape[3]).astype(jnp.float32)
+        here = pl.ds(piece * (depth // pieces), depth // pieces)
+        rows = 2 * depth // pieces
+        plain = plain_ref[chosen, here].reshape(rows, plain_ref.shape[3])
+        other = other_ref[chosen, here].reshape(rows, other_ref.shape[3]).astype(jnp.float32)
         even = lax.rem(lax.broadcasted_iota(jnp.int32, other.shape, 0), 2) == 0
         signed = jnp.where(even, other, -other).astype(jnp.bfloat16)
         swapped = jnp.where(even, pltpu.roll(other, rows - 1, 0), pltpu.roll(other, 1, 0)).astype(jnp.bfloat16)
@@ -293,11 +336,13 @@
         for p, factor in enumerate((signed, swapped)):
             product = lax.dot_general(plain, factor, dims, preferred_element_type=jnp.float32)
             product = product.reshape(n, span, columns)
-            if j == 0:
-                for b in range(n):
-                    at = sum((b >> s & 1) * (n >> (s + 1)) for s in range(steps))
+            for b in range(n if j == 0 else 0):
+                at = sum((b >> s & 1) * (n >> (s + 1)) for s in range(steps))
+                if piece:
+                    part[p, at] += product[b]
+                else:
                     part[p, at] = product[b]
-            else:
+            if j:
                 part[2 * j + p] = product
 
     def reduce_copy(c, s):
@@ -399,13 +444,13 @@
         for p in range(2):
             put(absorbed.at[p, :, core + 2 * side], absorbed_out.at[p, :, core + 2 * side], leaf_sem.at[low, p])
 
-    for copy in leaf_copies(0):
-        copy.start()
+    for piece in range(HALVES):
+        for copy in leaf_copies(0, piece, HALVES):
+            copy.start()
     own_copy.start()
-    leaf_product(0)
-    for j in LEAF_ORDER:
-        for copy in leaf_copies(j):
-            copy.start()
+    bits_copy.wait()
+    for piece in range(HALVES):
+        leaf_product(0, piece, HALVES)
     pl.semaphore_wait(barrier, n - 1)
 
     acts = dict(
@@ -480,9 +525,10 @@
             jax.ShapeDtypeStruct((2, 2 * width, width), jnp.bfloat16),
             jax.ShapeDtypeStruct((2, n // 4, 4, span, columns), jnp.bfloat16),
         ),
-        in_specs=[pl.BlockSpec(memory_space=pltpu.SMEM), anywhere, anywhere, anywhere],
+        in_specs=[anywhere, anywhere, anywhere, anywhere],
         out_specs=(anywhere, anywhere),
         scratch_shapes=[
+            pltpu.SMEM((branches,), jnp.int32),
             *[pltpu.VMEM((slices, depth, 2, rows), jnp.bfloat16)] * branches,
             *[pltpu.VMEM((slices, depth, 2, columns), jnp.bfloat16)] * branches,
             pltpu.VMEM(both, jnp.float32),

time: 91.2 us -> 89.7 us (0.984)
  Pallas kernels: 90.9 us -> 89 us
    pallas_call x1, Pallas kernels: 86.9 us -> 85.1 us  [on_device(): pl.pallas_call(functools.partial(network_kernel, n), out_shape=(jax.Shape...]
where the time goes in v3:
time: 89.7 us; the launch traced here: 89.2 us
  Pallas kernels  89 us (99%)
    pallas_call x1, Pallas kernels, on_device(): pl.pallas_call(functools.partial(network_kernel, n), out_shape=(jax.Shape...  85.1 us
    pallas_call x1, Pallas kernels, contract_last(): pl.pallas_call(last_kernel, out_shape=jax.ShapeDtypeStruct((rows // 2, 2,...  3.91 us

profile of v3, /device:TPU:1, one launch (start us, length us, event | category | flops | bytes accessed | tf_op | source)
XLA Modules:
  0.0 89.2 jit_solution(9603916667742408186)
XLA Ops:
  0.0 85.1 %shard_map.46 = (bf16[2,1024,512]{2,1,0:T(8,128)(2,1)}, bf16[2,4,4,32,512]{4,3,2,1,0:T(8,128)(2,1)}) custom-call(s32[4]{0:T(128)} %bits_in.1, bf16[16,32,2,512]{3,2,1,0:T(2,128)(2,1)} %bitcast.3, bf16[4,2,512,2,512]{4,3,2,1,0:T(2,128)(2,1)} %left.1, bf16[4,2,512,2,512]{4,3,2,1,0:T(2,128)(2,1)} %right.1), custom_call_target="tpu_custom_call" | custom-call | tf_op jit(solution)/shard_map/pallas_call | solution.py:522
  85.1 3.9 %shard_map.47 = bf16[512,2,512]{2,1,0:T(2,128)(2,1)} custom-call(bf16[2,1024,512]{2,1,0:T(8,128)(2,1)} %get-tuple-element.7.mixed, bf16[2,512,512]{2,1,0:T(8,128)(2,1)} %bitcast.4), custom_call_target="tpu_custom_call" | custom-call | tf_op jit(solution)/shard_map/pallas_call | solution.py:499

commit v4 on v3

--- a/solution.py
+++ b/solution.py
@@ -10,7 +10,7 @@
 MESH = pl.DeviceIdType.MESH
 LANES = 128
 TILES = 4
-HALVES = 1
+HALVES = 2
 LEAF_ORDER = (3, 2, 1)
 PIECES = (2, 1, 2, 1)
 
@@ -225,7 +225,7 @@
 
 def network_kernel(
     n, bits_in, stem, left, right, mixed_out, absorbed_out,
-    bits,    l0, l1, l2, l3, r0, r1, r2, r3, part, outgoing, incoming, branch, got0, planes, blocks1, got1, absorbed,
+    bits,    l0, l1, l2, l3, l4, r0, r1, r2, r3, r4, part, outgoing, incoming, branch, got0, planes, blocks1, got1, absorbed,
     q_product, mixed, wide, leaf_sem, own_sem, a_send, a_recv, r_send, r_recv,
 ):
     planes_in, _, span, columns = part.shape
@@ -235,7 +235,7 @@
     steps = n.bit_length() - 1
     group = n // 4
     me = lax.axis_index("outer")
-    lefts, rights = (l0, l1, l2, l3), (r0, r1, r2, r3)
+    lefts, rights = (l0, l1, l2, l3, l4), (r0, r1, r2, r3, r4)
 
     bit = [lax.rem(me // (1 << s), 2) for s in range(steps)]
 
@@ -263,13 +263,13 @@
     bits_copy = pltpu.make_async_copy(bits_in, bits, own_sem)
     bits_copy.start()
 
-    depth = l0.shape[1]
+    depth = l1.shape[1]
 
     def leaf_copies(j, piece=0, pieces=1):
         here = pl.ds(piece * (depth // pieces), depth // pieces)
         return (
-            pltpu.make_async_copy(left.at[j, :, here], lefts[j].at[:, here], leaf_sem.at[j + piece, 0]),
-            pltpu.make_async_copy(right.at[j, :, here], rights[j].at[:, here], leaf_sem.at[j + piece, 1]),
+            pltpu.make_async_copy(left.at[j, :, here], lefts[j + 4 * piece], leaf_sem.at[j + 4 * piece, 0]),
+            pltpu.make_async_copy(right.at[j, :, here], rights[j + 4 * piece], leaf_sem.at[j + 4 * piece, 1]),
         )
 
     def first_copy(k):
@@ -324,11 +324,11 @@
                 for copy in leaf_copies(other):
                     copy.start()
         chosen = bits[j]
-        plain_ref, other_ref = (rights[j], lefts[j]) if j % 2 == 0 else (lefts[j], rights[j])
-        here = pl.ds(piece * (depth // pieces), depth // pieces)
+        k = j + 4 * piece
+        plain_ref, other_ref = (rights[k], lefts[k]) if j % 2 == 0 else (lefts[k], rights[k])
         rows = 2 * depth // pieces
-        plain = plain_ref[chosen, here].reshape(rows, plain_ref.shape[3])
-        other = other_ref[chosen, here].reshape(rows, other_ref.shape[3]).astype(jnp.float32)
+        plain = plain_ref[chosen].reshape(rows, plain_ref.shape[3])
+        other = other_ref[chosen].reshape(rows, other_ref.shape[3]).astype(jnp.float32)
         even = lax.rem(lax.broadcasted_iota(jnp.int32, other.shape, 0), 2) == 0
         signed = jnp.where(even, other, -other).astype(jnp.bfloat16)
         swapped = jnp.where(even, pltpu.roll(other, rows - 1, 0), pltpu.roll(other, 1, 0)).astype(jnp.bfloat16)
@@ -519,6 +519,7 @@
     blocks = stem_tensor.reshape(n, span, 2, columns)
     both = (2 * branches, n, span, columns)
     anywhere = pl.BlockSpec(memory_space=pl.ANY)
+    sizes = [depth // HALVES, *[depth] * (branches - 1), depth // HALVES]
     mixed, absorbed = pl.pallas_call(
         functools.partial(network_kernel, n),
         out_shape=(
@@ -529,8 +530,8 @@
         out_specs=(anywhere, anywhere),
         scratch_shapes=[
             pltpu.SMEM((branches,), jnp.int32),
-            *[pltpu.VMEM((slices, depth, 2, rows), jnp.bfloat16)] * branches,
-            *[pltpu.VMEM((slices, depth, 2, columns), jnp.bfloat16)] * branches,
+            *[pltpu.VMEM((slices, size, 2, rows), jnp.bfloat16) for size in sizes],
+            *[pltpu.VMEM((slices, size, 2, columns), jnp.bfloat16) for size in sizes],
             pltpu.VMEM(both, jnp.float32),
             pltpu.VMEM(both, jnp.bfloat16),
             pltpu.VMEM(both, jnp.bfloat16),
@@ -543,7 +544,7 @@
             pltpu.VMEM((2, width, columns), jnp.bfloat16),
             pltpu.VMEM((2, 2 * width, columns), jnp.bfloat16),
             pltpu.VMEM((columns // LANES, 2 * width, LANES), jnp.float32),
-            pltpu.SemaphoreType.DMA((branches, 2)),
+            pltpu.SemaphoreType.DMA((branches + 1, 2)),
             pltpu.SemaphoreType.DMA,
             pltpu.SemaphoreType.DMA((n,)),
             pltpu.SemaphoreType.DMA((2, 4)),

time: 89.7 us -> 88.3 us (0.984)
  Pallas kernels: 89 us -> 87.8 us
    pallas_call x1, Pallas kernels: 85.1 us -> 83.9 us  [on_device(): pl.pallas_call(functools.partial(network_kernel, n), out_shape=(jax.Shape...]
where the time goes in v4:
time: 88.3 us; the launch traced here: 87.9 us
  Pallas kernels  87.8 us (99%)
    pallas_call x1, Pallas kernels, on_device(): pl.pallas_call(functools.partial(network_kernel, n), out_shape=(jax.Shape...  83.9 us
    pallas_call x1, Pallas kernels, contract_last(): pl.pallas_call(last_kernel, out_shape=jax.ShapeDtypeStruct((rows // 2, 2,...  3.91 us

profile of v4, /device:TPU:1, one launch (start us, length us, event | category | flops | bytes accessed | tf_op | source)
XLA Modules:
  0.0 87.9 jit_solution(10248188186969249362)
XLA Ops:
  0.0 83.9 %shard_map.46 = (bf16[2,1024,512]{2,1,0:T(8,128)(2,1)}, bf16[2,4,4,32,512]{4,3,2,1,0:T(8,128)(2,1)}) custom-call(s32[4]{0:T(128)} %bits_in.1, bf16[16,32,2,512]{3,2,1,0:T(2,128)(2,1)} %bitcast.3, bf16[4,2,512,2,512]{4,3,2,1,0:T(2,128)(2,1)} %left.1, bf16[4,2,512,2,512]{4,3,2,1,0:T(2,128)(2,1)} %right.1), custom_call_target="tpu_custom_call" | custom-call | tf_op jit(solution)/shard_map/pallas_call | solution.py:523
  83.9 3.9 %shard_map.47 = bf16[512,2,512]{2,1,0:T(2,128)(2,1)} custom-call(bf16[2,1024,512]{2,1,0:T(8,128)(2,1)} %get-tuple-element.7.mixed, bf16[2,512,512]{2,1,0:T(8,128)(2,1)} %bitcast.4), custom_call_target="tpu_custom_call" | custom-call | tf_op jit(solution)/shard_map/pallas_call | solution.py:499

commit v5 on v4

--- a/solution.py
+++ b/solution.py
@@ -19,14 +19,14 @@
 ENTRIES = (0.5, 15.0, 7.0, 20.0)
 GAP = 0.4
 TABLE = [
+    ('first', 15),
     ('first', 14),
     ('turn', 0, 0),
     ('turn', 3, 0),
+    ('turn', 1, 0),
     ('leaf', 3),
     ('turn', 2, 0),
-    ('first', 15),
     ('turn', 0, 1),
-    ('turn', 1, 0),
     ('first', 5),
     ('first', 12),
     ('first', 4),
@@ -57,6 +57,7 @@
     ('turn', 4, 1),
     ('turn', 7, 2),
     ('turn', 3, 3),
+    ('first', 6),
     ('turn', 10, 0),
     ('turn', 5, 1),
     ('turn', 8, 2),
@@ -79,12 +80,11 @@
     ('turn', 11, 2),
     ('turn', 9, 1),
     ('first', 2),
-    ('first', 6),
     ('turn', 4, 3),
     ('turn', 5, 3),
     ('turn', 3, 5),
+    ('turn', 6, 4),
     ('turn', 10, 1),
-    ('turn', 6, 4),
     ('turn', 2, 5),
     ('first', 13),
     ('turn', 1, 5),
@@ -97,8 +97,8 @@
     ('turn', 4, 4),
     ('turn', 8, 5),
     ('turn', 2, 6),
+    ('turn', 5, 4),
     ('turn', 10, 2),
-    ('turn', 5, 4),
     ('first', 11),
     ('turn', 0, 6),
     ('turn', 4, 5),
@@ -120,8 +120,8 @@
     ('turn', 0, 8),
     ('turn', 1, 7),
     ('split', 2),
+    ('turn', 7, 5),
     ('turn', 2, 8),
-    ('turn', 7, 5),
     ('split', 3),
     ('contract', 2),
     ('turn', 10, 4),
@@ -136,11 +136,11 @@
     ('second', 12),
     ('second', 8),
     ('turn', 7, 6),
-    ('contract', 1),
     ('turn', 11, 6),
     ('turn', 9, 5),
     ('turn', 10, 6),
     ('turn', 6, 7),
+    ('contract', 1),
     ('turn', 7, 7),
     ('turn', 8, 7),
     ('second', 6),
@@ -159,12 +159,12 @@
     ('turn', 10, 7),
     ('second', 7),
     ('second', 1),
-    ('turn', 11, 8),
     ('second', 2),
     ('second', 9),
     ('turn', 9, 7),
     ('turn', 10, 8),
     ('second', 3),
+    ('turn', 11, 8),
     ('turn', 6, 8),
     ('turn', 5, 8),
     ('multiply',),

time: 88.3 us -> 88.2 us (level)
  no operation moved by 1% of the time
where the time goes in v5:
time: 88.2 us; the launch traced here: 87.9 us
  Pallas kernels  87.8 us (100%)
    pallas_call x1, Pallas kernels, on_device(): pl.pallas_call(functools.partial(network_kernel, n), out_shape=(jax.Shape...  83.9 us
    pallas_call x1, Pallas kernels, contract_last(): pl.pallas_call(last_kernel, out_shape=jax.ShapeDtypeStruct((rows // 2, 2,...  3.91 us

profile of v5, /device:TPU:1, one launch (start us, length us, event | category | flops | bytes accessed | tf_op | source)
XLA Modules:
  0.0 87.9 jit_solution(9939864460981470741)
XLA Ops:
  0.0 83.9 %shard_map.46 = (bf16[2,1024,512]{2,1,0:T(8,128)(2,1)}, bf16[2,4,4,32,512]{4,3,2,1,0:T(8,128)(2,1)}) custom-call(s32[4]{0:T(128)} %bits_in.1, bf16[16,32,2,512]{3,2,1,0:T(2,128)(2,1)} %bitcast.3, bf16[4,2,512,2,512]{4,3,2,1,0:T(2,128)(2,1)} %left.1, bf16[4,2,512,2,512]{4,3,2,1,0:T(2,128)(2,1)} %right.1), custom_call_target="tpu_custom_call" | custom-call | tf_op jit(solution)/shard_map/pallas_call | solution.py:523
  83.9 3.9 %shard_map.47 = bf16[512,2,512]{2,1,0:T(2,128)(2,1)} custom-call(bf16[2,1024,512]{2,1,0:T(8,128)(2,1)} %get-tuple-element.7.mixed, bf16[2,512,512]{2,1,0:T(8,128)(2,1)} %bitcast.4), custom_call_target="tpu_custom_call" | custom-call | tf_op jit(solution)/shard_map/pallas_call | solution.py:499
